TPU v7x, 32 devices: a whole 2x2x4 slice. The times are simulated.
32 devices in a mesh: macro: 8 (over y, x, core), rve: 4 (over z).
Axes of the slice: x: 2, y: 2, z: 4, core: 2. Of those that a mesh axis runs over, the one named last changes fastest.
Arguments:
- deform: float32 [9, 512], P(None, 'macro'), may hold values from -6 to 6
- plastic: int32 [512], P('macro'), may hold values 0 or 1
- route: int32 [512], P('macro'), may hold values from 0 to 7, as said below
- stiff: float32 [8, 1536], P('macro', 'rve'), may hold values from 0.1 to 2
- cubic: float32 [8, 1536], P('macro', 'rve'), may hold values from 0.5 to 5
- coupling: float32 [8, 24, 2, 64, 64], P('macro', 'rve'), may hold values from -0.75 to 0.75
- conn: int32 [8, 24, 2], P('macro', 'rve'), may hold values from 0 to 5
- iface: float32 [8, 256, 64], P('macro', 'rve'), may hold values from -0.75 to 0.75
- load_map: float32 [8, 9, 1536], P('macro', None, 'rve'), may hold values from -2 to 2
- average_map: float32 [8, 9, 1536], P('macro', None, 'rve'), may hold values from -0.15625 to 0.15625
Outputs:
- stress: float32 [9, 512], P(None, 'macro')
- micro_field: float32 [8, 1536, 128], P('macro', 'rve')
Inputs may be any that keep to these rules, and one draw needn't show every extreme that they name: `route`: among the points of one macro section no group is named more than 16 times, and one group is named exactly 16 times by every section. `conn`: an index among the 6 blocks held with the same block row on one device.
All inputs are finite; a program needn't handle non-finite values. No bound on the sum of `plastic` on one device may be relied on, other than what follows from the above.
Results may differ from a plain program's by a relative error of at most 0.0003.
Values sent between devices are 32-bit elements; how exact they have to be, the bound alone decides.
A program may use at most 64 MiB of HBM per device.

v0:
```python
import jax
import jax.numpy as jnp
from jax import lax
from jax.sharding import PartitionSpec as P

ITERS = 2
NEWTON = 2


HIGHEST_PREC = lax.Precision.HIGHEST
EPSILON = 1e-06


def from_behind(block, axis, distance):
    devices = range(lax.axis_size(axis))
    route = [((i - distance) % len(devices), i) for i in devices]
    return lax.ppermute(block, axis, route)


def with_halo(block, sides, width):
    for axis, dim in sides:
        count = lax.axis_size(axis)
        forward = [(i, i + 1) for i in range(count - 1)]
        forward.append((count - 1, 0))
        backward = [(target, source) for source, target in forward]
        low = lax.ppermute(
            lax.slice_in_dim(block, block.shape[dim] - width, None, axis=dim), axis, forward
        )
        high = lax.ppermute(lax.slice_in_dim(block, 0, width, axis=dim), axis, backward)
        block = jnp.concatenate([low, block, high], axis=dim)
    return block


def slot_index(route_rows, capacity):
    point_count = route_rows.shape[0]
    position = jnp.arange(point_count, dtype=jnp.int32)
    same_group = route_rows[:, None] == route_rows[None, :]
    before = position[None, :] < position[:, None]
    rank_in = jnp.sum(
        jnp.where(jnp.logical_and(same_group, before), 1, 0).astype(jnp.int32), axis=1
    )
    return route_rows * capacity + rank_in


def local_matrix(coupling, conn, stiff):
    blocks, slot_count, block_size, _ = coupling.shape
    spring = jnp.einsum("bsxk,bsyk->bsxy", coupling, coupling, precision=HIGHEST_PREC)
    block_ids = jnp.arange(blocks, dtype=jnp.int32)
    own_mark = (block_ids[None, None, :] == block_ids[:, None, None]).astype(jnp.float32)
    far_mark = jnp.logical_and(
        block_ids[None, None, :] == conn[:, :, None], conn[:, :, None] != block_ids[:, None, None]
    ).astype(jnp.float32)
    weight = own_mark - far_mark
    pair_mark = jnp.einsum("bsk,bsl->bskl", weight, weight, precision=HIGHEST_PREC)
    assembled = jnp.einsum("bskl,bsxy->kxly", pair_mark, spring, precision=HIGHEST_PREC)
    assembled = assembled.reshape(blocks * block_size, blocks * block_size)
    return assembled + jnp.diag(stiff)


def norm_sum(values):
    return lax.psum(jnp.sum(values * values, axis=0), "rve")


def split_solve(strain, flag_cols, stiff, cubic, coupling, conn, iface, load_map):
    block_size = coupling.shape[3]
    local_part = local_matrix(coupling[0], conn[0], stiff[0])
    edge_block = iface[0]
    own_spring = jnp.einsum("xk,yk->xy", edge_block, edge_block, precision=HIGHEST_PREC)
    next_edge = from_behind(edge_block, "rve", -1)
    next_spring = jnp.einsum("xk,yk->xy", next_edge, next_edge, precision=HIGHEST_PREC)
    load_cols = jnp.einsum("ci,cp->ip", load_map[0], strain, precision=HIGHEST_PREC)
    hard = flag_cols * cubic[0][:, None]

    def operate(field):
        product = jnp.dot(
            local_part, field, precision=HIGHEST_PREC, preferred_element_type=jnp.float32
        )
        first_rows = field[:block_size]
        last_rows = field[-block_size:]
        end_rows = jnp.concatenate([first_rows, last_rows], axis=0)
        padded = with_halo(end_rows, (("rve", 0),), block_size)
        top_flux = jnp.dot(
            own_spring,
            first_rows - padded[:block_size],
            precision=HIGHEST_PREC,
            preferred_element_type=jnp.float32,
        )
        bottom = jnp.dot(
            next_spring,
            last_rows - padded[-block_size:],
            precision=HIGHEST_PREC,
            preferred_element_type=jnp.float32,
        )
        product = product.at[:block_size].add(top_flux)
        product = product.at[-block_size:].add(bottom)
        return product

    solution = jnp.zeros_like(load_cols)
    for newton_step in range(NEWTON):
        tangent_add = 3.0 * hard * solution * solution
        if newton_step == 0:
            right_side = load_cols
        else:
            right_side = load_cols - operate(solution) - hard * (solution * solution * solution)

        def sweep(turn_index, carried):
            iterate, residue, direct, norm_now = carried
            product = operate(direct) + tangent_add * direct
            curvature_col = lax.psum(jnp.sum(direct * product, axis=0), "rve")
            step_len = norm_now / (curvature_col + EPSILON)
            iterate = iterate + step_len * direct
            residue = residue - step_len * product
            norm_next = norm_sum(residue)
            direct = residue + norm_next / (norm_now + EPSILON) * direct
            return (iterate, residue, direct, norm_next)

        start = (jnp.zeros_like(right_side), right_side, right_side, norm_sum(right_side))
        iterate, residue, direct, norm_now = lax.fori_loop(0, ITERS, sweep, start)
        solution = solution + iterate
    return solution


def shards(deform, plastic, route, stiff, cubic, coupling, conn, iface, load_map, average_map):
    groups = lax.axis_size("macro")
    capacity = 2 * deform.shape[1] // groups
    columns = groups * capacity
    slot_ids = slot_index(route, capacity)
    places = jnp.arange(columns, dtype=jnp.int32)
    select = (slot_ids[:, None] == places[None, :]).astype(jnp.float32)
    outgoing = jnp.dot(
        deform, select, precision=HIGHEST_PREC, preferred_element_type=jnp.float32
    ).reshape(9, groups, capacity)
    flags_out = jnp.dot(
        plastic.astype(jnp.float32)[None, :],
        select,
        precision=HIGHEST_PREC,
        preferred_element_type=jnp.float32,
    ).reshape(1, groups, capacity)
    incoming, flags_in = (
        lax.all_to_all(outgoing, "macro", split_axis=1, concat_axis=1, tiled=True),
        lax.all_to_all(flags_out, "macro", split_axis=1, concat_axis=1, tiled=True),
    )
    strain = incoming.reshape(9, columns)
    flag_cols = flags_in.reshape(1, columns)
    solution = split_solve(strain, flag_cols, stiff, cubic, coupling, conn, iface, load_map)
    part_stress = jnp.einsum("ci,ip->cp", average_map[0], solution, precision=HIGHEST_PREC)
    group_stress = lax.psum(part_stress, "rve")
    returned_rows = lax.all_to_all(
        group_stress.reshape(9, groups, capacity), "macro", split_axis=1, concat_axis=1, tiled=True
    )
    stress = jnp.dot(
        returned_rows.reshape(9, columns),
        select.T,
        precision=HIGHEST_PREC,
        preferred_element_type=jnp.float32,
    )
    return (stress, solution[None])


def solution(mesh):
    return jax.shard_map(
        shards,
        mesh=mesh,
        in_specs=(
            P(None, "macro"),
            P("macro"),
            P("macro"),
            P("macro", "rve"),
            P("macro", "rve"),
            P("macro", "rve", None, None, None),
            P("macro", "rve", None),
            P("macro", "rve", None),
            P("macro", None, "rve"),
            P("macro", None, "rve"),
        ),
        out_specs=(P(None, "macro"), P("macro", "rve", None)),
        check_vma=False,
    )
```

profile of v0, /device:TPU:0, one launch (start us, length us, event | category | flops | bytes accessed | tf_op | source)
XLA Modules:
  0.0 195.9 jit_solution(6440798218701041127)
XLA Ops:
  0.7 0.9 select_reduce_fusion
  1.6 0.7 multiply_add_fusion.4
  2.2 1.7 fusion.23
  3.9 5.2 %all-to-all-start.1 = ((f32[1,8,16]{2,0,1:T(1,128)}), f32[1,8,16]{2,0,1:T(1,128)S(1)}, u32[]{:S(2)}, u32[]{:S(2)}) async-start(f32[1,8,16]{2,0,1:T(1,128)} %fusion.23), calls=%async_computation.1 | async-start | bytes 8192 | tf_op jit(solution)/shard_map/all_to_all | solution.py:141
  9.1 3.6 %collective-permute-start.4 = (f32[64,64]{1,0:T(8,128)}, f32[64,64]{1,0:T(8,128)S(1)}, u32[]{:S(2)}, u32[]{:S(2)}) collective-permute-start(f32[64,64]{1,0:T(8,128)} %bitcast.118), channel_id=1, source_target_pairs={{1,0},{2,1},{3,2},{0,3},{5,4},{6,5},{7,6},{4,7},{9,8},{10,9},{11,1... | collective-permute-start | bytes 49160 | tf_op jit(solution)/shard_map/ppermute | solution.py:17
  12.7 0.7 iota_compare_fusion.7
  13.4 0.7 convert_subtract_fusion
  14.1 0.7 convolution_bitcast_fusion.5
  14.8 1.5 convolution_bitcast_fusion.4
  16.5 0.4 reshape.237
  16.9 0.3 copy-done.4
  17.6 0.7 reshape.256
  18.3 4.2 %all-to-all-start = ((f32[8,1,144]{2,1,0:T(1,128)}), f32[8,1,144]{2,1,0:T(1,128)S(1)}, u32[]{:S(2)}, u32[]{:S(2)}) async-start(f32[8,1,144]{2,1,0:T(1,128)} %reshape.256), calls=%async_computation | async-start | bytes 16384 | tf_op jit(solution)/shard_map/all_to_all | solution.py:140
  22.8 0.6 broadcast.213
  23.4 0.7 reduce.29
  24.1 3.1 %all-to-all-done = f32[8,1,144]{2,1,0:T(1,128)S(1)} async-done(((f32[8,1,144]{2,1,0:T(1,128)}), f32[8,1,144]{2,1,0:T(1,128)S(1)}, u32[]{:S(2)}, u32[]{:S(2)}) %all-to-all-start) | async-done | bytes 4640 | tf_op jit(solution)/shard_map/all_to_all | solution.py:140
  27.2 0.6 broadcast.215
  27.8 0.7 reduce.30
  28.7 0.5 multiply_reduce_fusion.5
  29.3 8.8 %psum.65 = f32[128]{0:T(128)S(1)} all-reduce(f32[128]{0:T(128)S(1)} %get-tuple-element.577), channel_id=1, replica_groups=mesh['macro'=8,'rve'=4] {'rve'}, use_global_device_ids=true, to_apply=%region_2.3 | all-reduce | flops 128 | bytes 1024 | tf_op jit(solution)/shard_map/psum | solution.py:61
  38.3 54.1 %while.46 = (s32[]{:T(128)}, f32[384,128]{1,0:T(8,128)S(1)}, f32[384,128]{1,0:T(8,128)S(1)}, f32[384,128]{1,0:T(8,128)S(1)}, f32[128]{0:T(128)S(1)}, /*index=5*/...) while((s32[]{:T(128)}, f32[384,128]{1,0:T(8,128)S(1)}, ...), condition=%wide.region_8.9_spmd.clone, body=%wide.region_3.8_spmd.clone.sunk | while | flops 240042496 | bytes 3879119 | solution.py:118
  38.4 1.6 collective-permute-start
  40.0 2.3 %collective-permute-start.1 = (f32[64,128]{1,0:T(8,128)S(1)}, f32[64,128]{1,0:T(8,128)S(1)}, u32[]{:S(2)}, u32[]{:S(2)}) collective-permute-start(f32[64,128]{1,0:T(8,128)S(1)} %get-tuple-element.697), channel_id=1, source_target_pairs={{1,0},{2,1},{3,2},{0,3},{5,4},{6,5},{7,6},{4,7},{9,8},{10,9},{11,1... | collective-permute-start | bytes 98312 | tf_op jit(solution)/shard_map/while/body/eval_jaxpr/ppermute | solution.py:29
  42.3 0.6 fusion.98
  42.9 1.3 collective-permute-done
  44.7 11.9 %psum.76 = f32[128]{0:T(128)S(1)} all-reduce(f32[128]{0:T(128)S(1)} %multiply_reduce_fusion.10), channel_id=1, replica_groups=mesh['macro'=8,'rve'=4] {'rve'}, use_global_device_ids=true, to_apply=%region_5.5 | all-reduce | flops 128 | bytes 1024 | tf_op jit(solution)/shard_map/while/body/eval_jaxpr/psum | solution.py:109
  56.7 0.3 multiply_reduce_fusion.11
  56.9 8.4 %psum.77 = f32[128]{0:T(128)S(1)} all-reduce(f32[128]{0:T(128)S(1)} %get-tuple-element.700), channel_id=1, replica_groups=mesh['macro'=8,'rve'=4] {'rve'}, use_global_device_ids=true, to_apply=%region_7.7 | all-reduce | flops 128 | bytes 1024 | tf_op jit(solution)/shard_map/while/body/eval_jaxpr/psum | solution.py:61
  65.4 2.0 %collective-permute-start = (f32[64,128]{1,0:T(8,128)S(1)}, f32[64,128]{1,0:T(8,128)S(1)}, u32[]{:S(2)}, u32[]{:S(2)}) collective-permute-start(f32[64,128]{1,0:T(8,128)S(1)} %get-tuple-element.696), channel_id=1, source_target_pairs={{0,1},{1,2},{2,3},{3,0},{4,5},{5,6},{6,7},{7,4},{8,9},{9,10},{10,1... | collective-permute-start | bytes 98312 | tf_op jit(solution)/shard_map/while/body/eval_jaxpr/ppermute | solution.py:26
  67.4 1.9 collective-permute-start.1
  69.3 0.6 fusion.98
  69.9 1.3 collective-permute-done
  71.9 11.8 %psum.76 = f32[128]{0:T(128)S(1)} all-reduce(f32[128]{0:T(128)S(1)} %multiply_reduce_fusion.10), channel_id=1, replica_groups=mesh['macro'=8,'rve'=4] {'rve'}, use_global_device_ids=true, to_apply=%region_5.5 | all-reduce | flops 128 | bytes 1024 | tf_op jit(solution)/shard_map/while/body/eval_jaxpr/psum | solution.py:109
  83.7 0.3 multiply_reduce_fusion.11
  84.0 8.4 %psum.77 = f32[128]{0:T(128)S(1)} all-reduce(f32[128]{0:T(128)S(1)} %get-tuple-element.700), channel_id=1, replica_groups=mesh['macro'=8,'rve'=4] {'rve'}, use_global_device_ids=true, to_apply=%region_7.7 | all-reduce | flops 128 | bytes 1024 | tf_op jit(solution)/shard_map/while/body/eval_jaxpr/psum | solution.py:61
  92.4 2.0 %collective-permute-start.5 = (f32[64,128]{1,0:T(8,128)S(1)}, f32[64,128]{1,0:T(8,128)S(1)}, u32[]{:S(2)}, u32[]{:S(2)}) collective-permute-start(f32[64,128]{1,0:T(8,128)S(1)} %get-tuple-element.576), channel_id=1, source_target_pairs={{0,1},{1,2},{2,3},{3,0},{4,5},{5,6},{6,7},{7,4},{8,9},{9,10},{10,1... | collective-permute-start | bytes 98312 | tf_op jit(solution)/shard_map/ppermute | solution.py:26
  94.5 0.7 fusion.54
  95.3 1.9 collective-permute-start.6
  97.2 1.0 collective-permute-done.5
  98.2 0.3 convolution_add_fusion.1
  98.5 0.7 scatter-add.22
  99.3 0.3 convolution_add_fusion
  99.6 0.6 scatter-add.23
  100.7 12.1 %psum.66 = f32[128]{0:T(128)S(1)} all-reduce(f32[128]{0:T(128)S(1)} %get-tuple-element.566), channel_id=1, replica_groups=mesh['macro'=8,'rve'=4] {'rve'}, use_global_device_ids=true, to_apply=%region_10.11 | all-reduce | flops 128 | bytes 1024 | tf_op jit(solution)/shard_map/psum | solution.py:61
  112.8 54.0 %while.47 = (s32[]{:T(128)}, f32[384,128]{1,0:T(8,128)S(1)}, f32[384,128]{1,0:T(8,128)S(1)}, f32[384,128]{1,0:T(8,128)S(1)}, f32[128]{0:T(128)S(1)}, /*index=5*/...) while((s32[]{:T(128)}, f32[384,128]{1,0:T(8,128)S(1)}, ...), condition=%wide.region_16.17_spmd.clone, body=%wide.region_11.16_spmd.clone.sunk | while | flops 239845888 | bytes 4268231 | solution.py:118
  112.9 3.8 %collective-permute-start.3 = (f32[64,128]{1,0:T(8,128)S(1)}, f32[64,128]{1,0:T(8,128)S(1)}, u32[]{:S(2)}, u32[]{:S(2)}) collective-permute-start(f32[64,128]{1,0:T(8,128)S(1)} %get-tuple-element.711), channel_id=1, source_target_pairs={{1,0},{2,1},{3,2},{0,3},{5,4},{6,5},{7,6},{4,7},{9,8},{10,9},{11,1... | collective-permute-start | bytes 98312 | tf_op jit(solution)/shard_map/while/body/eval_jaxpr/ppermute | solution.py:29
  116.7 0.6 fusion.108
  117.3 1.2 collective-permute-done.2
  119.0 12.0 %psum.78 = f32[128]{0:T(128)S(1)} all-reduce(f32[128]{0:T(128)S(1)} %multiply_reduce_fusion.12), channel_id=1, replica_groups=mesh['macro'=8,'rve'=4] {'rve'}, use_global_device_ids=true, to_apply=%region_13.13 | all-reduce | flops 128 | bytes 1024 | tf_op jit(solution)/shard_map/while/body/eval_jaxpr/psum | solution.py:109
  131.2 8.4 %psum.79 = f32[128]{0:T(128)S(1)} all-reduce(f32[128]{0:T(128)S(1)} %get-tuple-element.714), channel_id=1, replica_groups=mesh['macro'=8,'rve'=4] {'rve'}, use_global_device_ids=true, to_apply=%region_15.15 | all-reduce | flops 128 | bytes 1024 | tf_op jit(solution)/shard_map/while/body/eval_jaxpr/psum | solution.py:61
  139.7 2.0 %collective-permute-start.2 = (f32[64,128]{1,0:T(8,128)S(1)}, f32[64,128]{1,0:T(8,128)S(1)}, u32[]{:S(2)}, u32[]{:S(2)}) collective-permute-start(f32[64,128]{1,0:T(8,128)S(1)} %get-tuple-element.710), channel_id=1, source_target_pairs={{0,1},{1,2},{2,3},{3,0},{4,5},{5,6},{6,7},{7,4},{8,9},{9,10},{10,1... | collective-permute-start | bytes 98312 | tf_op jit(solution)/shard_map/while/body/eval_jaxpr/ppermute | solution.py:26
  141.7 1.9 collective-permute-start.3
  143.6 0.6 fusion.108
  144.2 1.3 collective-permute-done.2
  145.7 0.3 collective-permute-done.3
  146.3 11.9 %psum.78 = f32[128]{0:T(128)S(1)} all-reduce(f32[128]{0:T(128)S(1)} %multiply_reduce_fusion.12), channel_id=1, replica_groups=mesh['macro'=8,'rve'=4] {'rve'}, use_global_device_ids=true, to_apply=%region_13.13 | all-reduce | flops 128 | bytes 1024 | tf_op jit(solution)/shard_map/while/body/eval_jaxpr/psum | solution.py:109
  158.3 8.4 %psum.79 = f32[128]{0:T(128)S(1)} all-reduce(f32[128]{0:T(128)S(1)} %get-tuple-element.714), channel_id=1, replica_groups=mesh['macro'=8,'rve'=4] {'rve'}, use_global_device_ids=true, to_apply=%region_15.15 | all-reduce | flops 128 | bytes 1024 | tf_op jit(solution)/shard_map/while/body/eval_jaxpr/psum | solution.py:61
  167.2 18.3 %psum.67 = f32[9,8,16]{2,0,1:T(8,128)S(1)} all-reduce(f32[9,8,16]{2,0,1:T(8,128)S(1)} %copy.105), channel_id=1, replica_groups=mesh['macro'=8,'rve'=4] {'rve'}, use_global_device_ids=true, to_apply=%region_17.18 | all-reduce | flops 1152 | bytes 9216 | tf_op jit(solution)/shard_map/psum | solution.py:147
  185.5 0.7 reshape.258
  186.2 3.3 %all-to-all-start.2 = ((f32[8,1,144]{2,1,0:T(1,128)}), f32[8,1,144]{2,1,0:T(1,128)S(1)}, u32[]{:S(2)}, u32[]{:S(2)}) async-start(f32[8,1,144]{2,1,0:T(1,128)} %reshape.258), calls=%async_computation.2 | async-start | bytes 16384 | tf_op jit(solution)/shard_map/all_to_all | solution.py:148
  189.5 0.7 add_bitcast_fusion
  190.2 3.9 %all-to-all-done.2 = f32[8,1,144]{2,1,0:T(1,128)S(1)} async-done(((f32[8,1,144]{2,1,0:T(1,128)}), f32[8,1,144]{2,1,0:T(1,128)S(1)}, u32[]{:S(2)}, u32[]{:S(2)}) %all-to-all-start.2) | async-done | bytes 4640 | tf_op jit(solution)/shard_map/all_to_all | solution.py:148
  194.1 0.7 reduce.31
  195.0 0.8 fusion.31
  (86 shorter events, 5.4 us)
Async XLA Ops:
  0.6 13.4 %copy-start = (f32[1,6,2,64,64]{4,3,2,1,0:T(8,128)S(1)}, f32[1,6,2,64,64]{4,3,2,1,0:T(8,128)}, u32[]{:S(2)}) copy-start(f32[1,6,2,64,64]{4,3,2,1,0:T(8,128)} %param.31) | copy-start | bytes 589828
  3.9 14.4 %all-to-all-start.1 = ((f32[1,8,16]{2,0,1:T(1,128)}), f32[1,8,16]{2,0,1:T(1,128)S(1)}, u32[]{:S(2)}, u32[]{:S(2)}) async-start(f32[1,8,16]{2,0,1:T(1,128)} %fusion.23), calls=%async_computation.1 | async-start | bytes 8192 | tf_op jit(solution)/shard_map/all_to_all | solution.py:141
  9.1 29.1 %collective-permute-start.4 = (f32[64,64]{1,0:T(8,128)}, f32[64,64]{1,0:T(8,128)S(1)}, u32[]{:S(2)}, u32[]{:S(2)}) collective-permute-start(f32[64,64]{1,0:T(8,128)} %bitcast.118), channel_id=1, source_target_pairs={{1,0},{2,1},{3,2},{0,3},{5,4},{6,5},{7,6},{4,7},{9,8},{10,9},{11,1... | collective-permute-start | bytes 49160 | tf_op jit(solution)/shard_map/ppermute | solution.py:17
  16.5 0.7 copy-start.4
  16.5 0.8 copy-start.6
  16.5 6.0 %copy-start.3 = (f32[1,64,64]{2,1,0:T(8,128)S(1)}, f32[1,64,64]{2,1,0:T(8,128)}, u32[]{:S(2)}) copy-start(f32[1,64,64]{2,1,0:T(8,128)} %param.33) | copy-start | bytes 49156
  16.5 6.2 %copy-start.5 = (f32[1,384]{1,0:T(1,128)S(1)}, f32[1,384]{1,0:T(1,128)}, u32[]{:S(2)}) copy-start(f32[1,384]{1,0:T(1,128)} %param.30) | copy-start | bytes 4612
  16.5 12.2 %copy-start.1 = (f32[1,9,384]{2,0,1:T(1,128)S(1)}, f32[1,9,384]{2,0,1:T(1,128)}, u32[]{:S(2)}) copy-start(f32[1,9,384]{2,0,1:T(1,128)} %param.34) | copy-start | bytes 41476
  18.3 8.9 %all-to-all-start = ((f32[8,1,144]{2,1,0:T(1,128)}), f32[8,1,144]{2,1,0:T(1,128)S(1)}, u32[]{:S(2)}, u32[]{:S(2)}) async-start(f32[8,1,144]{2,1,0:T(1,128)} %reshape.256), calls=%async_computation | async-start | bytes 16384 | tf_op jit(solution)/shard_map/all_to_all | solution.py:140
  38.4 5.8 %collective-permute-start = (f32[64,128]{1,0:T(8,128)S(1)}, f32[64,128]{1,0:T(8,128)S(1)}, u32[]{:S(2)}, u32[]{:S(2)}) collective-permute-start(f32[64,128]{1,0:T(8,128)S(1)} %get-tuple-element.696), channel_id=1, source_target_pairs={{0,1},{1,2},{2,3},{3,0},{4,5},{5,6},{6,7},{7,4},{8,9},{9,10},{10,1... | collective-permute-start | bytes 98312 | tf_op jit(solution)/shard_map/while/body/eval_jaxpr/ppermute | solution.py:26
  40.0 4.4 %collective-permute-start.1 = (f32[64,128]{1,0:T(8,128)S(1)}, f32[64,128]{1,0:T(8,128)S(1)}, u32[]{:S(2)}, u32[]{:S(2)}) collective-permute-start(f32[64,128]{1,0:T(8,128)S(1)} %get-tuple-element.697), channel_id=1, source_target_pairs={{1,0},{2,1},{3,2},{0,3},{5,4},{6,5},{7,6},{4,7},{9,8},{10,9},{11,1... | collective-permute-start | bytes 98312 | tf_op jit(solution)/shard_map/while/body/eval_jaxpr/ppermute | solution.py:29
  65.4 5.8 %collective-permute-start = (f32[64,128]{1,0:T(8,128)S(1)}, f32[64,128]{1,0:T(8,128)S(1)}, u32[]{:S(2)}, u32[]{:S(2)}) collective-permute-start(f32[64,128]{1,0:T(8,128)S(1)} %get-tuple-element.696), channel_id=1, source_target_pairs={{0,1},{1,2},{2,3},{3,0},{4,5},{5,6},{6,7},{7,4},{8,9},{9,10},{10,1... | collective-permute-start | bytes 98312 | tf_op jit(solution)/shard_map/while/body/eval_jaxpr/ppermute | solution.py:26
  67.4 4.1 %collective-permute-start.1 = (f32[64,128]{1,0:T(8,128)S(1)}, f32[64,128]{1,0:T(8,128)S(1)}, u32[]{:S(2)}, u32[]{:S(2)}) collective-permute-start(f32[64,128]{1,0:T(8,128)S(1)} %get-tuple-element.697), channel_id=1, source_target_pairs={{1,0},{2,1},{3,2},{0,3},{5,4},{6,5},{7,6},{4,7},{9,8},{10,9},{11,1... | collective-permute-start | bytes 98312 | tf_op jit(solution)/shard_map/while/body/eval_jaxpr/ppermute | solution.py:29
  92.4 5.8 %collective-permute-start.5 = (f32[64,128]{1,0:T(8,128)S(1)}, f32[64,128]{1,0:T(8,128)S(1)}, u32[]{:S(2)}, u32[]{:S(2)}) collective-permute-start(f32[64,128]{1,0:T(8,128)S(1)} %get-tuple-element.576), channel_id=1, source_target_pairs={{0,1},{1,2},{2,3},{3,0},{4,5},{5,6},{6,7},{7,4},{8,9},{9,10},{10,1... | collective-permute-start | bytes 98312 | tf_op jit(solution)/shard_map/ppermute | solution.py:26
  95.3 4.0 %collective-permute-start.6 = (f32[64,128]{1,0:T(8,128)S(1)}, f32[64,128]{1,0:T(8,128)S(1)}, u32[]{:S(2)}, u32[]{:S(2)}) collective-permute-start(f32[64,128]{1,0:T(8,128)S(1)} %get-tuple-element.575), channel_id=1, source_target_pairs={{1,0},{2,1},{3,2},{0,3},{5,4},{6,5},{7,6},{4,7},{9,8},{10,9},{11,1... | collective-permute-start | bytes 98312 | tf_op jit(solution)/shard_map/ppermute | solution.py:29
  112.8 54.0 %copy-start.2 = (f32[1,9,384]{2,0,1:T(1,128)S(1)}, f32[1,9,384]{2,0,1:T(1,128)}, u32[]{:S(2)}) copy-start(f32[1,9,384]{2,0,1:T(1,128)} %param.35) | copy-start | bytes 41476
  112.8 5.8 %collective-permute-start.2 = (f32[64,128]{1,0:T(8,128)S(1)}, f32[64,128]{1,0:T(8,128)S(1)}, u32[]{:S(2)}, u32[]{:S(2)}) collective-permute-start(f32[64,128]{1,0:T(8,128)S(1)} %get-tuple-element.710), channel_id=1, source_target_pairs={{0,1},{1,2},{2,3},{3,0},{4,5},{5,6},{6,7},{7,4},{8,9},{9,10},{10,1... | collective-permute-start | bytes 98312 | tf_op jit(solution)/shard_map/while/body/eval_jaxpr/ppermute | solution.py:26
  112.9 5.9 %collective-permute-start.3 = (f32[64,128]{1,0:T(8,128)S(1)}, f32[64,128]{1,0:T(8,128)S(1)}, u32[]{:S(2)}, u32[]{:S(2)}) collective-permute-start(f32[64,128]{1,0:T(8,128)S(1)} %get-tuple-element.711), channel_id=1, source_target_pairs={{1,0},{2,1},{3,2},{0,3},{5,4},{6,5},{7,6},{4,7},{9,8},{10,9},{11,1... | collective-permute-start | bytes 98312 | tf_op jit(solution)/shard_map/while/body/eval_jaxpr/ppermute | solution.py:29
  139.7 5.8 %collective-permute-start.2 = (f32[64,128]{1,0:T(8,128)S(1)}, f32[64,128]{1,0:T(8,128)S(1)}, u32[]{:S(2)}, u32[]{:S(2)}) collective-permute-start(f32[64,128]{1,0:T(8,128)S(1)} %get-tuple-element.710), channel_id=1, source_target_pairs={{0,1},{1,2},{2,3},{3,0},{4,5},{5,6},{6,7},{7,4},{8,9},{9,10},{10,1... | collective-permute-start | bytes 98312 | tf_op jit(solution)/shard_map/while/body/eval_jaxpr/ppermute | solution.py:26
  141.7 4.3 %collective-permute-start.3 = (f32[64,128]{1,0:T(8,128)S(1)}, f32[64,128]{1,0:T(8,128)S(1)}, u32[]{:S(2)}, u32[]{:S(2)}) collective-permute-start(f32[64,128]{1,0:T(8,128)S(1)} %get-tuple-element.711), channel_id=1, source_target_pairs={{1,0},{2,1},{3,2},{0,3},{5,4},{6,5},{7,6},{4,7},{9,8},{10,9},{11,1... | collective-permute-start | bytes 98312 | tf_op jit(solution)/shard_map/while/body/eval_jaxpr/ppermute | solution.py:29
  186.2 8.0 %all-to-all-start.2 = ((f32[8,1,144]{2,1,0:T(1,128)}), f32[8,1,144]{2,1,0:T(1,128)S(1)}, u32[]{:S(2)}, u32[]{:S(2)}) async-start(f32[8,1,144]{2,1,0:T(1,128)} %reshape.258), calls=%async_computation.2 | async-start | bytes 16384 | tf_op jit(solution)/shard_map/all_to_all | solution.py:148
where the time goes:
time: 197 us; the launch traced here: 196 us
  blocking collectives  120 us (61%)
  starting transfers between devices  35.7 us (18%)
  waiting for transfers between devices  13.8 us (7%)
  matrix products  11.2 us (6%)
  other arithmetic  7.84 us (4%)
  local copies, waits for them, and re-layouts  5.78 us (3%)
    psum x6, blocking collectives, norm_sum(): return lax.psum(jnp.sum(values * values, axis=0), 'rve')  54.4 us
    psum x4, blocking collectives, sweep(): curvature_col = lax.psum(jnp.sum(direct * product, axis=0), 'rve')  47.6 us
    psum x1, blocking collectives, shards(): group_stress = lax.psum(part_stress, 'rve')  18.3 us
    ppermute x5, starting transfers between devices, with_halo(): lax.ppermute(lax.slice_in_dim(block, 0, width, axis=dim), axis, backward)  11.7 us
    ppermute x5, starting transfers between devices, with_halo(): lax.ppermute(lax.slice_in_dim(block, block.shape[dim] - width, None, axis...  7.7 us
    ppermute x5, waiting for transfers between devices, with_halo(): lax.ppermute(lax.slice_in_dim(block, block.shape[dim] - width, None, axis...  6.12 us
    all_to_all x1, starting transfers between devices, shards(): lax.all_to_all(flags_out, 'macro', split_axis=1, concat_axis=1, tiled=True)  5.17 us
    all_to_all x1, starting transfers between devices, shards(): lax.all_to_all(outgoing, 'macro', split_axis=1, concat_axis=1, tiled=True)  4.2 us
  transfers between devices with their start and end apart: 14, of which 10 were waited for; matrix products, arithmetic and copies ran while one was open for 7% of the time, Pallas kernels for 0%

commit v1 on v0

v1 whole, which is shorter than its diff:
```python
import functools

import jax
import jax.numpy as jnp
from jax import lax
from jax.experimental import pallas as pl
from jax.experimental.pallas import tpu as pltpu
from jax.sharding import PartitionSpec as P

EPSILON = 1e-06
MESH = pl.DeviceIdType.MESH
HIGHEST = lax.Precision.HIGHEST
F32 = jnp.float32
BF16 = jnp.bfloat16
LANES = 128
NT = (((1,), (1,)), ((), ()))


def split(values):
    high = values.astype(BF16)
    return high, (values - high.astype(F32)).astype(BF16)


def dot(left, right):
    return jnp.dot(left, right, preferred_element_type=F32)


def dot_nt(left, right, precision=None):
    return lax.dot_general(left, right, NT, precision=precision, preferred_element_type=F32)


def apply_split(high, low, values):
    value_high, value_low = split(values)
    width = values.shape[1]
    wide = dot(high, jnp.concatenate([value_high, value_low], axis=1))
    return wide[:, :width] + wide[:, width:] + dot(low, value_high)


def square_nt(values):
    high, low = split(values)
    return dot_nt(high, high) + (dot_nt(high, low) + dot_nt(low, high))


def iota(shape, dim):
    return lax.broadcasted_iota(jnp.int32, shape, dim)


def pad_rows(values, rows):
    missing = rows - values.shape[0]
    if missing == 0:
        return values
    return jnp.concatenate([values, jnp.zeros((missing, values.shape[1]), values.dtype)], axis=0)


def col_sum(values):
    return jnp.sum(values, axis=0, keepdims=True)


def kernel(
    groups, parts, capacity,
    deform_ref, plastic_ref, route_ref, stiff_ref, cubic_ref, coupling_ref, conn_ref,
    iface_ref, load_ref, average_ref,
    stress_ref, field_ref,
    factor_high, factor_low, stiff_high, stiff_low,
    out_points, in_points, edge_out, edge_in,
    halo_out, halo_in, sum_buf, part_buf, out_rows, in_rows,
    point_send, point_recv, edge_send, edge_recv, halo_send, halo_recv,
    sum_send, sum_recv, part_send, part_recv, row_send, row_recv,
):
    group = lax.axis_index("macro")
    part = lax.axis_index("rve")
    blocks, slots, block = coupling_ref.shape[1], coupling_ref.shape[2], coupling_ref.shape[3]
    dofs = blocks * block
    points = deform_ref.shape[1]
    comps = deform_ref.shape[0]
    padded = out_points.shape[1]
    columns = groups * capacity
    places = groups * padded

    barrier = pltpu.get_barrier_semaphore()
    for step in range(1, groups):
        pl.semaphore_signal(
            barrier, inc=1, device_id={"macro": lax.rem(group + step, groups)}, device_id_type=MESH
        )
    for step in range(1, parts):
        pl.semaphore_signal(
            barrier, inc=1, device_id={"rve": lax.rem(part + step, parts)}, device_id_type=MESH
        )

    route = route_ref[...]
    hot = (iota((groups, points), 0) == route).astype(F32)
    before = (iota((points, points), 0) < iota((points, points), 1)).astype(BF16)
    rank = col_sum(hot * dot(hot.astype(BF16), before))
    slot = (route * padded).astype(F32) + rank
    select = (iota((places, points), 0).astype(F32) == slot).astype(F32)
    sent = jnp.concatenate(
        [deform_ref[...], plastic_ref[...].astype(F32)], axis=0
    )
    sent = pad_rows(sent, LANES)
    outgoing = dot_nt(select, sent, HIGHEST)
    out_points[...] = outgoing.reshape(groups, padded, LANES)

    maps = pad_rows(jnp.concatenate([load_ref[0], cubic_ref[...]], axis=0), 16)
    edge_out[0:16, :] = jnp.concatenate([maps[:, :block], maps[:, dofs - block:]], axis=1)
    own_edge = iface_ref[0]
    edge_out[16:, :] = jnp.concatenate([own_edge, jnp.zeros((block, LANES - block), F32)], axis=1)

    pl.semaphore_wait(barrier, groups + parts - 2)

    def exchange(source, target, send, recv):
        copies = []
        for step in range(1, groups):
            peer = lax.rem(group + step, groups)
            copies.append(pltpu.make_async_remote_copy(
                src_ref=source.at[peer], dst_ref=target.at[group],
                send_sem=send.at[step - 1], recv_sem=recv.at[step - 1],
                device_id={"macro": peer}, device_id_type=MESH,
            ))
            copies[-1].start()
        return copies

    def share(buffer, send, recv):
        copies = []
        for step in range(1, parts):
            copies.append(pltpu.make_async_remote_copy(
                src_ref=buffer.at[part], dst_ref=buffer.at[part],
                send_sem=send.at[step - 1], recv_sem=recv.at[step - 1],
                device_id={"rve": lax.rem(part + step, parts)}, device_id_type=MESH,
            ))
            copies[-1].start()
        return copies

    after, behind = lax.rem(part + 1, parts), lax.rem(part + parts - 1, parts)

    def to_neighbours(first, last, target, send, recv):
        copies = []
        for place, (source, peer) in enumerate(((last, after), (first, behind))):
            copies.append(pltpu.make_async_remote_copy(
                src_ref=source, dst_ref=target.at[place],
                send_sem=send.at[place], recv_sem=recv.at[place],
                device_id={"rve": peer}, device_id_type=MESH,
            ))
            copies[-1].start()
        return copies

    def arrive(copies):
        for copy in copies:
            copy.wait_recv()

    sends = []
    point_copies = exchange(out_points, in_points, point_send, point_recv)
    edge_copies = to_neighbours(edge_out, edge_out, edge_in, edge_send, edge_recv)
    sends += point_copies + edge_copies
    in_points[group] = out_points[group]

    lane = iota((block, LANES), 1)
    for row in range(blocks):
        pair = jnp.concatenate([coupling_ref[0, row, 0], coupling_ref[0, row, 1]], axis=1)
        high, low = split(pair)
        for near in range(blocks):
            rows = slice(near * block, (near + 1) * block)
            cols = slice(row * LANES, (row + 1) * LANES)
            if near == row:
                factor_high[rows, cols] = high
                factor_low[rows, cols] = low
            else:
                first = jnp.where(conn_ref[0, row, 0] == near, -1.0, 0.0).astype(F32)
                second = jnp.where(conn_ref[0, row, 1] == near, -1.0, 0.0).astype(F32)
                mark = jnp.where(lane < block, first, second).astype(BF16)
                factor_high[rows, cols] = high * mark
                factor_low[rows, cols] = low * mark
    fh, fl = factor_high[...], factor_low[...]
    stiffness = dot_nt(fh, fh) + (dot_nt(fh, fl) + dot_nt(fl, fh))
    diagonal = iota((dofs, dofs), 0) == iota((dofs, dofs), 1)
    stiffness = stiffness + jnp.where(diagonal, stiff_ref[...], 0.0)
    own_spring = square_nt(own_edge)
    own_high, own_low = split(own_spring)
    maps_cols = jnp.transpose(maps)
    average = pad_rows(average_ref[0], 16)
    average_high, average_low = split(average)

    arrive(edge_copies)
    next_spring = square_nt(edge_in[1, 16:, :][:, :block])
    next_high, next_low = split(next_spring)
    high, low = split(stiffness)
    stiff_high[...] = high
    stiff_low[...] = low
    high, low = split(stiffness[:block, :block] + own_spring)
    stiff_high[:block, :block] = high
    stiff_low[:block, :block] = low
    high, low = split(stiffness[dofs - block:, dofs - block:] + next_spring)
    stiff_high[dofs - block:, dofs - block:] = high
    stiff_low[dofs - block:, dofs - block:] = low
    prev_maps = jnp.transpose(edge_in[0, 0:16, :])[block:]
    next_maps = jnp.transpose(edge_in[1, 0:16, :])[:block]
    ghost_maps = jnp.concatenate([prev_maps, next_maps], axis=0)

    arrive(point_copies)

    def compact(rows):
        rows = rows.reshape(places, LANES)
        if padded == capacity:
            return rows
        row, col = iota((columns, places), 0), iota((columns, places), 1)
        take = (col == (row // capacity) * padded + row % capacity).astype(F32)
        return jnp.dot(take, rows, precision=HIGHEST, preferred_element_type=F32)

    strain = jnp.transpose(compact(in_points[...]))[:16]
    flag = strain[comps:comps + 1]
    strain_only = jnp.where(iota((16, columns), 0) < comps, strain, 0.0)
    load = jnp.dot(maps_cols, strain_only, precision=HIGHEST, preferred_element_type=F32)
    ghost_load = jnp.dot(ghost_maps, strain_only, precision=HIGHEST, preferred_element_type=F32)
    hard = maps_cols[:, comps:comps + 1] * flag
    ghost_hard = ghost_maps[:, comps:comps + 1] * flag

    def local(values):
        return apply_split(stiff_high[...], stiff_low[...], values)

    def coupled(product, ghost):
        top = product[:block] - apply_split(own_high, own_low, ghost[:block])
        bottom = product[dofs - block:] - apply_split(next_high, next_low, ghost[block:])
        return jnp.concatenate([top, product[block:dofs - block], bottom], axis=0)

    def start_sum(turn, values):
        sum_buf[turn, part] = pad_rows(jnp.concatenate(values, axis=0), 8)
        return share(sum_buf.at[turn], sum_send.at[turn], sum_recv.at[turn])

    def end_sum(turn, copies):
        arrive(copies)
        total = sum_buf[turn, 0]
        for other in range(1, parts):
            total = total + sum_buf[turn, other]
        return total

    def start_halo(turn, values):
        halo_out[turn, 0] = values[:block]
        halo_out[turn, 1] = values[dofs - block:]
        return to_neighbours(
            halo_out.at[turn, 0], halo_out.at[turn, 1], halo_in.at[turn],
            halo_send.at[turn], halo_recv.at[turn],
        )

    def end_halo(turn, copies):
        arrive(copies)
        return halo_in[turn].reshape(2 * block, columns)

    residue, ghost = load, ghost_load
    solved = None
    turn = 0
    for newton in range(2):
        image = coupled(local(residue), ghost)
        if newton == 1:
            image = image + tangent * residue
        halo_copies = start_halo(turn, image)
        sum_copies = start_sum(2 * newton, [col_sum(residue * residue), col_sum(residue * image)])
        sends += halo_copies + sum_copies
        second = local(image)
        ghost_image = end_halo(turn, halo_copies)
        turn += 1
        second = coupled(second, ghost_image)
        if newton == 1:
            second = second + tangent * image
        else:
            second_copies = start_halo(turn, second)
            sends += second_copies
        sums = end_sum(2 * newton, sum_copies)
        norm, curve = sums[0:1], sums[1:2]
        step_len = norm / (curve + EPSILON)
        left = residue - step_len * image
        left_image = image - step_len * second
        sum_copies = start_sum(
            2 * newton + 1,
            [col_sum(left * left), col_sum(left * left_image), col_sum(left * image)],
        )
        sends += sum_copies
        sums = end_sum(2 * newton + 1, sum_copies)
        left_norm, left_curve, cross = sums[0:1], sums[1:2], sums[2:3]
        ratio = left_norm / (norm + EPSILON)
        next_curve = left_curve + ratio * (2.0 * cross + ratio * curve)
        next_len = left_norm / (next_curve + EPSILON)
        from_start = step_len + next_len * ratio
        change = from_start * residue + next_len * left
        if newton == 0:
            solved = change
            hard_square = hard * solved * solved
            tangent = 3.0 * hard_square
            new_residue = load - (from_start * image + next_len * left_image) - hard_square * solved
            ghost_second = end_halo(turn, second_copies)
            turn += 1
            ghost_left = ghost - step_len * ghost_image
            ghost_left_image = ghost_image - step_len * ghost_second
            ghost_solved = from_start * ghost + next_len * ghost_left
            ghost = (
                ghost_load - (from_start * ghost_image + next_len * ghost_left_image)
                - ghost_hard * ghost_solved * ghost_solved * ghost_solved
            )
            residue = new_residue
        else:
            solved = solved + change

    part_buf[part] = apply_split(average_high, average_low, solved)
    part_copies = share(part_buf, part_send, part_recv)
    field_ref[0] = solved
    arrive(part_copies)
    total = part_buf[0]
    for other in range(1, parts):
        total = total + part_buf[other]
    rows = jnp.transpose(pad_rows(total, LANES))
    if padded != capacity:
        row, col = iota((places, columns), 0), iota((places, columns), 1)
        spread = jnp.logical_and(
            col == (row // padded) * capacity + row % padded, row % padded < capacity
        ).astype(F32)
        rows = jnp.dot(spread, rows, precision=HIGHEST, preferred_element_type=F32)
    out_rows[...] = rows.reshape(groups, padded, LANES)
    row_copies = exchange(out_rows, in_rows, row_send, row_recv)
    sends += part_copies + row_copies
    in_rows[group] = out_rows[group]
    arrive(row_copies)
    back = jnp.transpose(in_rows[...].reshape(places, LANES))[:16]
    picked = jnp.dot(back, select, precision=HIGHEST, preferred_element_type=F32)
    stress_ref[...] = picked[:comps]
    for copy in sends:
        copy.wait_send()


def solution(mesh):
    groups, parts = mesh.shape["macro"], mesh.shape["rve"]

    def shards(deform, plastic, route, stiff, cubic, coupling, conn, iface, load_map, average_map):
        comps, points = deform.shape
        blocks, block = coupling.shape[1], coupling.shape[3]
        dofs = blocks * block
        capacity = 2 * points // groups
        columns = groups * capacity
        padded = -(-capacity // 8) * 8
        vmem = pl.BlockSpec(memory_space=pltpu.VMEM)
        dma = pltpu.SemaphoreType.DMA
        return pl.pallas_call(
            functools.partial(kernel, groups, parts, capacity),
            out_shape=(
                jax.ShapeDtypeStruct((comps, points), F32),
                jax.ShapeDtypeStruct((1, dofs, columns), F32),
            ),
            in_specs=[vmem] * 6 + [pl.BlockSpec(memory_space=pltpu.SMEM)] + [vmem] * 3,
            out_specs=(vmem, vmem),
            scratch_shapes=[
                pltpu.VMEM((dofs, blocks * LANES), BF16),
                pltpu.VMEM((dofs, blocks * LANES), BF16),
                pltpu.VMEM((dofs, dofs), BF16),
                pltpu.VMEM((dofs, dofs), BF16),
                pltpu.VMEM((groups, padded, LANES), F32),
                pltpu.VMEM((groups, padded, LANES), F32),
                pltpu.VMEM((16 + block, LANES), F32),
                pltpu.VMEM((2, 16 + block, LANES), F32),
                pltpu.VMEM((3, 2, block, columns), F32),
                pltpu.VMEM((3, 2, block, columns), F32),
                pltpu.VMEM((4, parts, 8, columns), F32),
                pltpu.VMEM((parts, 16, columns), F32),
                pltpu.VMEM((groups, padded, LANES), F32),
                pltpu.VMEM((groups, padded, LANES), F32),
                dma((groups - 1,)), dma((groups - 1,)),
                dma((2,)), dma((2,)),
                dma((3, 2)), dma((3, 2)),
                dma((4, parts - 1)), dma((4, parts - 1)),
                dma((parts - 1,)), dma((parts - 1,)),
                dma((groups - 1,)), dma((groups - 1,)),
            ],
            compiler_params=pltpu.CompilerParams(
                collective_id=0, has_side_effects=True, vmem_limit_bytes=32 * 1024 * 1024
            ),
        )(
            deform, plastic[None], route[None], stiff, cubic, coupling, conn,
            iface, load_map, average_map,
        )

    return jax.shard_map(
        shards,
        mesh=mesh,
        in_specs=(
            P(None, "macro"),
            P("macro"),
            P("macro"),
            P("macro", "rve"),
            P("macro", "rve"),
            P("macro", "rve", None, None, None),
            P("macro", "rve", None),
            P("macro", "rve", None),
            P("macro", None, "rve"),
            P("macro", None, "rve"),
        ),
        out_specs=(P(None, "macro"), P("macro", "rve", None)),
        check_vma=False,
    )
```

time: 197 us -> 42.7 us (0.22)
  blocking collectives: 120 us -> 0 us
  Pallas kernels: 0 us -> 37.2 us
  starting transfers between devices: 35.7 us -> 0 us
  waiting for transfers between devices: 13.8 us -> 0 us
  matrix products: 11.2 us -> 0 us
  other arithmetic: 7.84 us -> 0 us
    psum x11 -> x0, blocking collectives: 120 us -> none  [the longest x6 54.4 us: norm_sum(): return lax.psum(jnp.sum(values * values, axis=0), 'rve')]
    pallas_call x0 -> x1, Pallas kernels: none -> 37.2 us  [shards(): pl.pallas_call(functools.partial(kernel, groups, parts, capacity), out_sh...]
    ppermute x11 -> x0, starting transfers between devices: 23 us -> none  [the longest x5 11.7 us: with_halo(): lax.ppermute(lax.slice_in_dim(block, 0, width, axis=dim), axis, backward)]
    all_to_all x3 -> x0, starting transfers between devices: 12.7 us -> none  [the longest x1 5.17 us: shards(): lax.all_to_all(flags_out, 'macro', split_axis=1, concat_axis=1, tiled=True)]
    dot_general x24 -> x0, matrix products: 11.2 us -> none  [the longest x5 3.26 us: operate(): jnp.dot(local_part, field, precision=HIGHEST_PREC, preferred_element_type...]
    all_to_all x3 -> x0, waiting for transfers between devices: 7.02 us -> none  [the longest x1 3.94 us: shards(): lax.all_to_all(group_stress.reshape(9, groups, capacity), 'macro', split_...]
    ppermute x11 -> x0, waiting for transfers between devices: 6.75 us -> none  [the longest x5 6.12 us: with_halo(): lax.ppermute(lax.slice_in_dim(block, block.shape[dim] - width, None, axis...]
    reduce_sum x10 -> x0, other arithmetic: 2.49 us -> none  [the longest x5 1.17 us: norm_sum(): return lax.psum(jnp.sum(values * values, axis=0), 'rve')]
  transfers between devices with their start and end apart: 14 -> 0, of which waited for: 10 -> 0; matrix products, arithmetic and copies ran while one was open for 7% -> 0% of each run, Pallas kernels for 0% -> 0%
where the time goes in v1:
time: 42.7 us; the launch traced here: 42.3 us
  Pallas kernels  37.2 us (87%)
  local copies, waits for them, and re-layouts  4.44 us (10%)
  between operations  0.7 us (2%)
    pallas_call x1, Pallas kernels, shards(): pl.pallas_call(functools.partial(kernel, groups, parts, capacity), out_sh...  37.2 us
    unnamed x23, local copies, waits for them, and re-layouts  4.44 us

profile of v1, /device:TPU:0, one launch (start us, length us, event | category | flops | bytes accessed | tf_op | source)
XLA Modules:
  0.0 42.3 jit_solution(16935772340258165289)
XLA Ops:
  0.6 0.0 copy-start.8
  0.6 0.7 %copy-done.8 = s32[1,6,2]{1,2,0:T(2,128)S(1)} copy-done((s32[1,6,2]{1,2,0:T(2,128)S(1)}, s32[1,6,2]{1,2,0:T(2,128)}, u32[]{:S(2)}) %copy-start.8) | copy-done | bytes 72
  1.3 0.0 copy-start.7
  1.3 0.1 copy.12.conn_ref
  1.4 0.0 copy-start.1
  1.4 0.7 %copy.13.load_ref = f32[1,9,384]{2,1,0:T(8,128)S(1)} copy(f32[1,9,384]{2,0,1:T(1,128)} %param.18) | data formatting | bytes 27648 | tf_op args[8]
  2.1 0.0 copy-done.7
  2.1 0.0 copy-start.2
  2.1 0.0 copy-start.3
  2.1 0.0 copy-start.4
  2.1 0.0 copy-start.5
  2.2 0.0 copy-start.6
  2.2 0.0 copy-done.1
  2.2 0.6 %copy-done.2 = f32[9,64]{1,0:T(8,128)S(1)} copy-done((f32[9,64]{1,0:T(8,128)S(1)}, f32[9,64]{1,0:T(8,128)}, u32[]{:S(2)}) %copy-start.2) | copy-done | bytes 2328
  2.8 0.0 copy-done.3
  2.8 0.0 copy-done.4
  2.8 0.0 copy-done.5
  2.9 0.0 copy-done.6
  2.9 0.0 copy-start
  2.9 1.0 %copy-done = f32[1,6,2,64,64]{4,3,2,1,0:T(8,128)S(1)} copy-done((f32[1,6,2,64,64]{4,3,2,1,0:T(8,128)S(1)}, f32[1,6,2,64,64]{4,3,2,1,0:T(8,128)}, u32[]{:S(2)}) %copy-start) | copy-done | bytes 196632
  3.9 37.2 %shard_map.113 = (f32[9,64]{1,0:T(8,128)S(1)}, f32[1,384,128]{2,1,0:T(8,128)S(1)}) custom-call(f32[9,64]{1,0:T(8,128)S(1)} %copy-done.2, s32[1,64]{1,0:T(1,128)S(1)} %bitcast.2, s32[1,64]{1,0:T(1,128)S(1)} %bitcast.3, f32[1,384]{1,0:T(1,128)S(1)} %copy-done.3, f32[1,384]{1,0:T(1,128)S(1)} %copy-done.4, f32[1,6,2,64,64]{4,3,2,1,0:T(8,128)S(1)} %copy-done, ...), custom_call_target="tpu_custom_call" | custom-call | tf_op jit(solution)/shard_map/pallas_call | solution.py:339
  41.0 0.6 %copy.17 = f32[9,64]{1,0:T(8,128)} copy(f32[9,64]{1,0:T(8,128)S(1)} %get-tuple-element.4) | data formatting | bytes 4608
  41.6 0.7 %copy.18 = f32[1,384,128]{2,1,0:T(8,128)} copy(f32[1,384,128]{2,1,0:T(8,128)S(1)} %get-tuple-element.5) | data formatting | bytes 393216
  (1 shorter events, 0.0 us)
Async XLA Ops:
  0.6 0.7 %copy-start.8 = (s32[1,6,2]{1,2,0:T(2,128)S(1)}, s32[1,6,2]{1,2,0:T(2,128)}, u32[]{:S(2)}) copy-start(s32[1,6,2]{1,2,0:T(2,128)} %param.16) | copy-start | bytes 148
  1.3 0.8 %copy-start.7 = (f32[1,9,384]{2,0,1:T(1,128)S(1)}, f32[1,9,384]{2,0,1:T(1,128)}, u32[]{:S(2)}) copy-start(f32[1,9,384]{2,0,1:T(1,128)} %param.19) | copy-start | bytes 41476
  1.4 0.8 %copy-start.1 = (f32[1,64,64]{2,1,0:T(8,128)S(1)}, f32[1,64,64]{2,1,0:T(8,128)}, u32[]{:S(2)}) copy-start(f32[1,64,64]{2,1,0:T(8,128)} %iface_ref.1) | copy-start | bytes 49156
  2.1 0.7 %copy-start.2 = (f32[9,64]{1,0:T(8,128)S(1)}, f32[9,64]{1,0:T(8,128)}, u32[]{:S(2)}) copy-start(f32[9,64]{1,0:T(8,128)} %deform_ref.1) | copy-start | bytes 6916
  2.1 0.7 %copy-start.3 = (f32[1,384]{1,0:T(1,128)S(1)}, f32[1,384]{1,0:T(1,128)}, u32[]{:S(2)}) copy-start(f32[1,384]{1,0:T(1,128)} %stiff_ref.1) | copy-start | bytes 4612
  2.1 0.7 %copy-start.4 = (f32[1,384]{1,0:T(1,128)S(1)}, f32[1,384]{1,0:T(1,128)}, u32[]{:S(2)}) copy-start(f32[1,384]{1,0:T(1,128)} %cubic_ref.1) | copy-start | bytes 4612
  2.1 0.7 %copy-start.5 = (s32[64]{0:T(128)S(1)}, s32[64]{0:T(128)}, u32[]{:S(2)}) copy-start(s32[64]{0:T(128)} %param.11) | copy-start | bytes 772
  2.2 0.7 %copy-start.6 = (s32[64]{0:T(128)S(1)}, s32[64]{0:T(128)}, u32[]{:S(2)}) copy-start(s32[64]{0:T(128)} %param.12) | copy-start | bytes 772
  2.9 1.0 %copy-start = (f32[1,6,2,64,64]{4,3,2,1,0:T(8,128)S(1)}, f32[1,6,2,64,64]{4,3,2,1,0:T(8,128)}, u32[]{:S(2)}) copy-start(f32[1,6,2,64,64]{4,3,2,1,0:T(8,128)} %coupling_ref.1) | copy-start | bytes 589828

commit v2 on v1

v2 whole, which is shorter than its diff:
```python
import functools

import jax
import jax.numpy as jnp
from jax import lax
from jax.experimental import pallas as pl
from jax.experimental.pallas import tpu as pltpu
from jax.sharding import PartitionSpec as P

EPSILON = 1e-06
MESH = pl.DeviceIdType.MESH
HIGHEST = lax.Precision.HIGHEST
F32 = jnp.float32
BF16 = jnp.bfloat16
LANES = 128
NT = (((1,), (1,)), ((), ()))


def split(values):
    high = values.astype(BF16)
    return high, (values - high.astype(F32)).astype(BF16)


def dot(left, right):
    return jnp.dot(left, right, preferred_element_type=F32)


def dot_nt(left, right, precision=None):
    return lax.dot_general(left, right, NT, precision=precision, preferred_element_type=F32)


def apply_split(high, low, values):
    value_high, value_low = split(values)
    width = values.shape[1]
    wide = dot(high, jnp.concatenate([value_high, value_low], axis=1))
    return wide[:, :width] + wide[:, width:] + dot(low, value_high)


def apply_rows(values, high, low):
    value_high, value_low = split(values)
    rows = values.shape[0]
    tall = dot(jnp.concatenate([value_high, value_low], axis=0), high)
    return tall[:rows] + tall[rows:] + dot(value_high, low)


def square_nt(values):
    high, low = split(values)
    return dot_nt(high, high) + (dot_nt(high, low) + dot_nt(low, high))


def iota(shape, dim):
    return lax.broadcasted_iota(jnp.int32, shape, dim)


def pad_rows(values, rows):
    missing = rows - values.shape[0]
    if missing == 0:
        return values
    return jnp.concatenate([values, jnp.zeros((missing, values.shape[1]), values.dtype)], axis=0)


def col_sum(values):
    return jnp.sum(values, axis=0, keepdims=True)


def kernel(
    groups, parts, capacity,
    deform_hbm, plastic_hbm, route_hbm, stiff_hbm, cubic_hbm, coupling_hbm, conn_ref,
    iface_hbm, load_hbm, average_hbm,
    stress_ref, field_ref,
    deform_ref, plastic_ref, route_ref, stiff_ref, cubic_ref, coupling_ref,
    iface_ref, load_ref, average_ref,
    whole, stiff_high, stiff_low,
    out_points, in_points, edge_out, edge_in,
    halo_out, halo_in, gram_buf, first_buf, second_buf, out_rows, in_rows,
    input_sem,
    point_send, point_recv, edge_send, edge_recv, halo_send, halo_recv,
    gram_send, gram_recv, first_send, first_recv, second_send, second_recv, row_send, row_recv,
):
    group = lax.axis_index("macro")
    part = lax.axis_index("rve")
    blocks, slots, block = coupling_ref.shape[1], coupling_ref.shape[2], coupling_ref.shape[3]
    dofs = blocks * block
    comps, points = deform_ref.shape
    padded = out_points.shape[1]
    columns = groups * capacity
    places = groups * padded

    barrier = pltpu.get_barrier_semaphore()
    for step in range(1, parts):
        pl.semaphore_signal(
            barrier, inc=1, device_id={"rve": lax.rem(part + step, parts)}, device_id_type=MESH
        )
    for step in range(1, groups):
        pl.semaphore_signal(
            barrier, inc=1, device_id={"macro": lax.rem(group + step, groups)}, device_id_type=MESH
        )

    loads = []
    for source, target in (
        (coupling_hbm, coupling_ref), (iface_hbm, iface_ref), (load_hbm, load_ref),
        (cubic_hbm, cubic_ref), (stiff_hbm, stiff_ref), (deform_hbm, deform_ref),
        (plastic_hbm, plastic_ref), (route_hbm, route_ref), (average_hbm, average_ref),
    ):
        loads.append(pltpu.make_async_copy(source, target, input_sem.at[len(loads)]))
        loads[-1].start()
    for copy in loads:
        copy.wait()

    def exchange(source, target, send, recv):
        copies = []
        for step in range(1, groups):
            peer = lax.rem(group + step, groups)
            copies.append(pltpu.make_async_remote_copy(
                src_ref=source.at[peer], dst_ref=target.at[group],
                send_sem=send.at[step - 1], recv_sem=recv.at[step - 1],
                device_id={"macro": peer}, device_id_type=MESH,
            ))
            copies[-1].start()
        return copies

    def share(buffer, send, recv):
        copies = []
        for step in range(1, parts):
            copies.append(pltpu.make_async_remote_copy(
                src_ref=buffer.at[part], dst_ref=buffer.at[part],
                send_sem=send.at[step - 1], recv_sem=recv.at[step - 1],
                device_id={"rve": lax.rem(part + step, parts)}, device_id_type=MESH,
            ))
            copies[-1].start()
        return copies

    after, behind = lax.rem(part + 1, parts), lax.rem(part + parts - 1, parts)

    def to_neighbours(first, last, target, send, recv):
        copies = []
        for place, (source, peer) in enumerate(((last, after), (first, behind))):
            copies.append(pltpu.make_async_remote_copy(
                src_ref=source, dst_ref=target.at[place],
                send_sem=send.at[place], recv_sem=recv.at[place],
                device_id={"rve": peer}, device_id_type=MESH,
            ))
            copies[-1].start()
        return copies

    def arrive(copies):
        for copy in copies:
            copy.wait_recv()

    def gathered(buffer):
        total = buffer[0]
        for other in range(1, parts):
            total = total + buffer[other]
        return total

    lane = iota((block, LANES), 1) < block
    doubled = []
    for row in range(blocks):
        square = square_nt(coupling_ref[0, row].reshape(slots * block, block))
        doubled.append([])
        for slot in range(slots):
            spring = square[slot * block:(slot + 1) * block, slot * block:(slot + 1) * block]
            doubled[row].append(jnp.concatenate([spring, spring], axis=1))

    def mark(row, slot, far):
        if row == far:
            return jnp.float32(0.0)
        return jnp.where(conn_ref[0, slot, row] == far, 1.0, 0.0).astype(F32)

    for row in range(blocks):
        own = doubled[row][0]
        for slot in range(1, slots):
            own = own + doubled[row][slot]
        for other in range(blocks):
            if other != row:
                for slot in range(slots):
                    own = own + doubled[other][slot] * mark(other, slot, row)
        for pair in range(blocks // 2):
            left, right = 2 * pair, 2 * pair + 1
            value = jnp.zeros((block, LANES), F32)
            for slot in range(slots):
                value = value - doubled[row][slot] * jnp.where(
                    lane, mark(row, slot, left), mark(row, slot, right)
                )
                value = value - jnp.where(
                    lane, doubled[left][slot] * mark(left, slot, row),
                    doubled[right][slot] * mark(right, slot, row),
                )
            if row == left:
                value = value + jnp.where(lane, own, 0.0)
            if row == right:
                value = value + jnp.where(lane, 0.0, own)
            whole[row * block:(row + 1) * block, pair * LANES:(pair + 1) * LANES] = value

    own_edge = iface_ref[0]
    own_spring = square_nt(own_edge)
    own_high, own_low = split(own_spring)
    diagonal = iota((dofs, dofs), 0) == iota((dofs, dofs), 1)
    stiffness = whole[...] + jnp.where(diagonal, stiff_ref[...], 0.0)
    high, low = split(stiffness)
    stiff_high[...] = high
    stiff_low[...] = low
    high, low = split(stiffness[:block, :block] + own_spring)
    stiff_high[:block, :block] = high
    stiff_low[:block, :block] = low

    maps = pad_rows(load_ref[:, 0, :], 16)
    cubic = pad_rows(cubic_ref[...], 16)

    def ends(values):
        return jnp.concatenate([values[:, :block], values[:, dofs - block:]], axis=1)

    image_map = apply_rows(maps, stiff_high[...], stiff_low[...])
    edge_out[0:16, :] = ends(maps)
    edge_out[16:32, :] = ends(image_map)
    edge_out[32:48, :] = ends(cubic)
    edge_out[48:, :] = jnp.concatenate([own_edge[:block // 2], own_edge[block // 2:]], axis=1)

    pl.semaphore_wait(barrier, groups + parts - 2)

    sends = []
    edge_copies = to_neighbours(edge_out, edge_out, edge_in, edge_send, edge_recv)

    route = route_ref[...]
    hot = (iota((groups, points), 0) == route).astype(F32)
    before = (iota((points, points), 0) < iota((points, points), 1)).astype(BF16)
    rank = col_sum(hot * dot(hot.astype(BF16), before))
    slot_of = (route * padded).astype(F32) + rank
    select = (iota((places, points), 0).astype(F32) == slot_of).astype(F32)
    sent = pad_rows(
        jnp.concatenate([deform_ref[...], plastic_ref[...].astype(F32)], axis=0), LANES
    )
    outgoing = dot_nt(select, sent, HIGHEST)
    out_points[...] = outgoing.reshape(groups, padded, LANES)
    point_copies = exchange(out_points, in_points, point_send, point_recv)
    sends += point_copies + edge_copies
    in_points[group] = out_points[group]
    average_high, average_low = split(pad_rows(average_ref[:, 0, :], 16))

    arrive(edge_copies)
    packed = edge_in[1, 48:, :]
    next_spring = square_nt(jnp.concatenate([packed[:, :block], packed[:, block:]], axis=0))
    next_high, next_low = split(next_spring)
    high, low = split(stiffness[dofs - block:, dofs - block:] + next_spring)
    stiff_high[dofs - block:, dofs - block:] = high
    stiff_low[dofs - block:, dofs - block:] = low

    def own_rows(values):
        return apply_rows(values, own_high, own_low)

    def next_rows(values):
        return apply_rows(values, next_high, next_low)

    prev_edge, next_edge = edge_in[0], edge_in[1]
    prev_map, next_map = prev_edge[0:16, block:], next_edge[0:16, :block]
    first_map, last_map = maps[:, :block], maps[:, dofs - block:]
    through_own = own_rows(jnp.concatenate([prev_map, first_map], axis=0))
    through_next = next_rows(jnp.concatenate([next_map, last_map], axis=0))
    prev_image = prev_edge[16:32, block:] + through_own[:16] - through_own[16:]
    next_image = next_edge[16:32, :block] - through_next[16:]
    image_map = jnp.concatenate([
        image_map[:, :block] - through_own[:16],
        image_map[:, block:dofs - block],
        image_map[:, dofs - block:] + through_next[16:] - through_next[:16],
    ], axis=1)
    second_map = apply_rows(image_map, stiff_high[...], stiff_low[...])
    second_map = jnp.concatenate([
        second_map[:, :block] - own_rows(prev_image),
        second_map[:, block:dofs - block],
        second_map[:, dofs - block:] - next_rows(next_image),
    ], axis=1)
    basis = jnp.concatenate([maps, image_map, second_map, cubic], axis=0)
    gram_buf[part, 0:32] = dot_nt(
        basis[0:32], jnp.concatenate([basis[0:48], jnp.zeros((LANES - 48, dofs), F32)], axis=0),
        HIGHEST,
    )
    gram_buf[part, 32:48] = ends(second_map)
    gram_copies = share(gram_buf, gram_send, gram_recv)
    sends += gram_copies

    basis_cols = jnp.transpose(basis)
    arrive(point_copies)

    def compact(rows):
        rows = rows.reshape(places, LANES)
        if padded == capacity:
            return rows
        row, col = iota((columns, places), 0), iota((columns, places), 1)
        take = (col == (row // capacity) * padded + row % capacity).astype(F32)
        return jnp.dot(take, rows, precision=HIGHEST, preferred_element_type=F32)

    received = jnp.transpose(compact(in_points[...]))[:16]
    flag = received[comps:comps + 1]
    strain = jnp.where(iota((16, columns), 0) < comps, received, 0.0)
    hard = basis_cols[:, 48:49] * flag

    arrive(gram_copies)
    ghost_basis = jnp.concatenate([
        jnp.concatenate([prev_map, next_map], axis=1),
        jnp.concatenate([prev_image, next_image], axis=1),
        jnp.concatenate(
            [gram_buf[behind, 32:48][:, block:], gram_buf[after, 32:48][:, :block]], axis=1
        ),
        jnp.concatenate([prev_edge[32:48, block:], next_edge[32:48, :block]], axis=1),
    ], axis=0)
    ghost_cols = jnp.transpose(ghost_basis)
    ghost_hard = ghost_cols[:, 48:49] * flag
    gram = gathered(gram_buf)
    forms = jnp.concatenate(
        [gram[0:16, 0:16], gram[0:16, 16:32], gram[16:32, 16:32], gram[16:32, 32:48]], axis=0
    )
    forms = jnp.dot(forms, strain, precision=HIGHEST, preferred_element_type=F32)
    norm = col_sum(forms[0:16] * strain)
    curve = col_sum(forms[16:32] * strain)
    third = col_sum(forms[32:48] * strain)
    fourth = col_sum(forms[48:64] * strain)

    def second_step(norm, curve, left_norm, left_curve, cross):
        ratio = left_norm / (norm + EPSILON)
        next_curve = left_curve + ratio * (2.0 * cross + ratio * curve)
        next_curve = jnp.maximum(next_curve, 0.09 * left_norm)
        next_len = left_norm / (next_curve + EPSILON)
        return next_len, next_len * ratio

    step_len = norm / (curve + EPSILON)
    left_norm = jnp.maximum(norm - step_len * (2.0 * curve - step_len * third), 0.0)
    left_curve = curve - step_len * (2.0 * third - step_len * fourth)
    cross = curve - step_len * third
    next_len, carried = second_step(norm, curve, left_norm, left_curve, cross)
    along = step_len + carried + next_len
    across = next_len * step_len
    zero = jnp.zeros_like(strain)
    weights = jnp.concatenate([
        jnp.concatenate([along * strain, -across * strain, zero], axis=0),
        jnp.concatenate([strain, -along * strain, across * strain], axis=0),
    ], axis=1)
    both = jnp.dot(
        jnp.concatenate([basis_cols[:, :48], ghost_cols[:, :48]], axis=0), weights,
        precision=HIGHEST, preferred_element_type=F32,
    )
    solved = both[:dofs, :columns]
    hard_square = hard * solved * solved
    tangent = 3.0 * hard_square
    residue = both[:dofs, columns:] - hard_square * solved
    ghost_solved = both[dofs:, :columns]
    ghost = both[dofs:, columns:] - ghost_hard * ghost_solved * ghost_solved * ghost_solved

    def coupled(product, ghost):
        top = product[:block] - apply_split(own_high, own_low, ghost[:block])
        bottom = product[dofs - block:] - apply_split(next_high, next_low, ghost[block:])
        return jnp.concatenate([top, product[block:dofs - block], bottom], axis=0)

    def averaged(values):
        return apply_split(average_high, average_low, values)[:comps]

    image = coupled(apply_split(stiff_high[...], stiff_low[...], residue), ghost)
    image = image + tangent * residue
    halo_out[0] = image[:block]
    halo_out[1] = image[dofs - block:]
    halo_copies = to_neighbours(
        halo_out.at[0], halo_out.at[1], halo_in, halo_send, halo_recv
    )
    first_buf[part] = pad_rows(jnp.concatenate([
        averaged(solved), averaged(residue), averaged(image),
        col_sum(residue * residue), col_sum(residue * image),
    ], axis=0), first_buf.shape[1])
    first_copies = share(first_buf, first_send, first_recv)
    sends += halo_copies + first_copies
    second = apply_split(stiff_high[...], stiff_low[...], image)
    arrive(first_copies)
    sums = gathered(first_buf)
    norm, curve = sums[3 * comps:3 * comps + 1], sums[3 * comps + 1:3 * comps + 2]
    step_len = norm / (curve + EPSILON)
    left = residue - step_len * image
    arrive(halo_copies)
    second = coupled(second, halo_in[...].reshape(2 * block, columns)) + tangent * image
    left_image = image - step_len * second
    second_buf[part] = pad_rows(jnp.concatenate(
        [col_sum(left * left), col_sum(left * left_image), col_sum(left * image)], axis=0
    ), 8)
    second_copies = share(second_buf, second_send, second_recv)
    sends += second_copies
    arrive(second_copies)
    last = gathered(second_buf)
    next_len, carried = second_step(norm, curve, last[0:1], last[1:2], last[2:3])
    along = step_len + carried
    total = (
        sums[:comps] + along * sums[comps:2 * comps]
        + next_len * (sums[comps:2 * comps] - step_len * sums[2 * comps:3 * comps])
    )

    rows = jnp.transpose(pad_rows(total, LANES))
    if padded != capacity:
        row, col = iota((places, columns), 0), iota((places, columns), 1)
        spread = jnp.logical_and(
            col == (row // padded) * capacity + row % padded, row % padded < capacity
        ).astype(F32)
        rows = jnp.dot(spread, rows, precision=HIGHEST, preferred_element_type=F32)
    out_rows[...] = rows.reshape(groups, padded, LANES)
    row_copies = exchange(out_rows, in_rows, row_send, row_recv)
    sends += row_copies
    in_rows[group] = out_rows[group]
    field_ref[0] = solved + along * residue + next_len * left
    arrive(row_copies)
    back = jnp.transpose(in_rows[...].reshape(places, LANES))[:16]
    picked = jnp.dot(back, select, precision=HIGHEST, preferred_element_type=F32)
    stress_ref[...] = picked[:comps]
    for copy in sends:
        copy.wait_send()


def solution(mesh):
    groups, parts = mesh.shape["macro"], mesh.shape["rve"]

    def shards(deform, plastic, route, stiff, cubic, coupling, conn, iface, load_map, average_map):
        comps, points = deform.shape
        blocks, block = coupling.shape[1], coupling.shape[3]
        dofs = blocks * block
        capacity = 2 * points // groups
        columns = groups * capacity
        padded = -(-capacity // 8) * 8
        vmem = pl.BlockSpec(memory_space=pltpu.VMEM)
        hbm = pl.BlockSpec(memory_space=pltpu.HBM)
        dma = pltpu.SemaphoreType.DMA
        return pl.pallas_call(
            functools.partial(kernel, groups, parts, capacity),
            out_shape=(
                jax.ShapeDtypeStruct((comps, points), F32),
                jax.ShapeDtypeStruct((1, dofs, columns), F32),
            ),
            in_specs=[hbm] * 6 + [pl.BlockSpec(memory_space=pltpu.SMEM)] + [hbm] * 3,
            out_specs=(vmem, vmem),
            scratch_shapes=[
                pltpu.VMEM(deform.shape, F32),
                pltpu.VMEM((1, points), jnp.int32),
                pltpu.VMEM((1, points), jnp.int32),
                pltpu.VMEM((1, dofs), F32),
                pltpu.VMEM((1, dofs), F32),
                pltpu.VMEM(coupling.shape, F32),
                pltpu.VMEM(iface.shape, F32),
                pltpu.VMEM((comps, 1, dofs), F32),
                pltpu.VMEM((comps, 1, dofs), F32),
                pltpu.VMEM((dofs, dofs), F32),
                pltpu.VMEM((dofs, dofs), BF16),
                pltpu.VMEM((dofs, dofs), BF16),
                pltpu.VMEM((groups, padded, LANES), F32),
                pltpu.VMEM((groups, padded, LANES), F32),
                pltpu.VMEM((48 + block // 2, LANES), F32),
                pltpu.VMEM((2, 48 + block // 2, LANES), F32),
                pltpu.VMEM((2, block, columns), F32),
                pltpu.VMEM((2, block, columns), F32),
                pltpu.VMEM((parts, 48, LANES), F32),
                pltpu.VMEM((parts, 32, columns), F32),
                pltpu.VMEM((parts, 8, columns), F32),
                pltpu.VMEM((groups, padded, LANES), F32),
                pltpu.VMEM((groups, padded, LANES), F32),
                dma((9,)),
                dma((groups - 1,)), dma((groups - 1,)),
                dma((2,)), dma((2,)),
                dma((2,)), dma((2,)),
                dma((parts - 1,)), dma((parts - 1,)),
                dma((parts - 1,)), dma((parts - 1,)),
                dma((parts - 1,)), dma((parts - 1,)),
                dma((groups - 1,)), dma((groups - 1,)),
            ],
            compiler_params=pltpu.CompilerParams(
                collective_id=0, has_side_effects=True, vmem_limit_bytes=60 * 1024 * 1024
            ),
        )(
            deform, plastic[None], route[None], stiff, cubic, coupling,
            jnp.transpose(conn, (0, 2, 1)), iface,
            jnp.transpose(load_map, (1, 0, 2)), jnp.transpose(average_map, (1, 0, 2)),
        )

    return jax.shard_map(
        shards,
        mesh=mesh,
        in_specs=(
            P(None, "macro"),
            P("macro"),
            P("macro"),
            P("macro", "rve"),
            P("macro", "rve"),
            P("macro", "rve", None, None, None),
            P("macro", "rve", None),
            P("macro", "rve", None),
            P("macro", None, "rve"),
            P("macro", None, "rve"),
        ),
        out_specs=(P(None, "macro"), P("macro", "rve", None)),
        check_vma=False,
    )
```

time: 42.7 us -> 34.4 us (0.81)
  Pallas kernels: 37.2 us -> 30.6 us
  local copies, waits for them, and re-layouts: 4.44 us -> 2.91 us
    pallas_call x1, Pallas kernels: 37.2 us -> 30.6 us  [shards(): pl.pallas_call(functools.partial(kernel, groups, parts, capacity), out_sh...]
    unnamed x23 -> x2, local copies, waits for them, and re-layouts: 4.44 us -> 2.91 us
where the time goes in v2:
time: 34.4 us; the launch traced here: 34.1 us
  Pallas kernels  30.6 us (89%)
  local copies, waits for them, and re-layouts  2.91 us (8%)
  between operations  0.64 us (2%)
    pallas_call x1, Pallas kernels, shards(): pl.pallas_call(functools.partial(kernel, groups, parts, capacity), out_sh...  30.6 us
    unnamed x2, local copies, waits for them, and re-layouts  2.91 us

profile of v2, /device:TPU:0, one launch (start us, length us, event | category | flops | bytes accessed | tf_op | source)
XLA Modules:
  0.0 34.1 jit_solution(18314022630560770617)
XLA Ops:
  0.6 30.6 %shard_map.113 = (f32[9,64]{1,0:T(8,128)}, f32[1,384,128]{2,1,0:T(8,128)}) custom-call(f32[9,64]{1,0:T(8,128)} %deform_hbm.1, s32[1,64]{1,0:T(1,128)} %bitcast.8, s32[1,64]{1,0:T(1,128)} %bitcast.9, f32[1,384]{1,0:T(1,128)} %stiff_hbm.1, f32[1,384]{1,0:T(1,128)} %cubic_hbm.1, f32[1,6,2,64,64]{4,3,2,1,0:T(8,128)} %coupling_hbm.1, s32[1,2,6]{2,1,0:T(2,128)} %bitcast.7, ...), custom_call_target="tpu_custom_call" | custom-call | tf_op jit(solution)/shard_map/pallas_call | solution.py:425
  31.2 1.3 %copy.14 = f32[9,64]{1,0:T(8,128)} copy(f32[9,64]{1,0:T(8,128)} %get-tuple-element.4) | data formatting | bytes 4608
  32.5 1.6 %copy.15 = f32[1,384,128]{2,1,0:T(8,128)} copy(f32[1,384,128]{2,1,0:T(8,128)} %get-tuple-element.5) | data formatting | bytes 393216

commit v3 on v2

--- a/solution.py
+++ b/solution.py
@@ -72,10 +72,10 @@
     iface_ref, load_ref, average_ref,
     whole, stiff_high, stiff_low,
     out_points, in_points, edge_out, edge_in,
-    halo_out, halo_in, gram_buf, first_buf, second_buf, out_rows, in_rows,
-    input_sem,
+    halo_out, halo_in, gram_buf, first_buf, mean_buf, second_buf, out_rows, in_rows, field_buf,
+    input_sem, output_sem,
     point_send, point_recv, edge_send, edge_recv, halo_send, halo_recv,
-    gram_send, gram_recv, first_send, first_recv, second_send, second_recv, row_send, row_recv,
+    gram_send, gram_recv, first_send, first_recv, mean_send, mean_recv, second_send, second_recv, row_send, row_recv,
 ):
     group = lax.axis_index("macro")
     part = lax.axis_index("rve")
@@ -104,8 +104,8 @@
     ):
         loads.append(pltpu.make_async_copy(source, target, input_sem.at[len(loads)]))
         loads[-1].start()
-    for copy in loads:
-        copy.wait()
+    coupling_load, iface_load = loads[:2]
+    early_loads, late_loads = loads[2:5], loads[5:]
 
     def exchange(source, target, send, recv):
         copies = []
@@ -153,6 +153,7 @@
             total = total + buffer[other]
         return total
 
+    coupling_load.wait()
     lane = iota((block, LANES), 1) < block
     doubled = []
     for row in range(blocks):
@@ -192,6 +193,9 @@
                 value = value + jnp.where(lane, 0.0, own)
             whole[row * block:(row + 1) * block, pair * LANES:(pair + 1) * LANES] = value
 
+    iface_load.wait()
+    for copy in early_loads:
+        copy.wait()
     own_edge = iface_ref[0]
     own_spring = square_nt(own_edge)
     own_high, own_low = split(own_spring)
@@ -221,6 +225,8 @@
     sends = []
     edge_copies = to_neighbours(edge_out, edge_out, edge_in, edge_send, edge_recv)
 
+    for copy in late_loads:
+        copy.wait()
     route = route_ref[...]
     hot = (iota((groups, points), 0) == route).astype(F32)
     before = (iota((points, points), 0) < iota((points, points), 1)).astype(BF16)
@@ -361,15 +367,18 @@
         halo_out.at[0], halo_out.at[1], halo_in, halo_send, halo_recv
     )
     first_buf[part] = pad_rows(jnp.concatenate([
-        averaged(solved), averaged(residue), averaged(image),
         col_sum(residue * residue), col_sum(residue * image),
     ], axis=0), first_buf.shape[1])
     first_copies = share(first_buf, first_send, first_recv)
-    sends += halo_copies + first_copies
     second = apply_split(stiff_high[...], stiff_low[...], image)
+    mean_buf[part] = pad_rows(jnp.concatenate(
+        [averaged(solved), averaged(residue), averaged(image)], axis=0
+    ), mean_buf.shape[1])
+    mean_copies = share(mean_buf, mean_send, mean_recv)
+    sends += halo_copies + first_copies + mean_copies
     arrive(first_copies)
     sums = gathered(first_buf)
-    norm, curve = sums[3 * comps:3 * comps + 1], sums[3 * comps + 1:3 * comps + 2]
+    norm, curve = sums[0:1], sums[1:2]
     step_len = norm / (curve + EPSILON)
     left = residue - step_len * image
     arrive(halo_copies)
@@ -380,13 +389,15 @@
     ), 8)
     second_copies = share(second_buf, second_send, second_recv)
     sends += second_copies
+    arrive(mean_copies)
+    means = gathered(mean_buf)
     arrive(second_copies)
     last = gathered(second_buf)
     next_len, carried = second_step(norm, curve, last[0:1], last[1:2], last[2:3])
     along = step_len + carried
     total = (
-        sums[:comps] + along * sums[comps:2 * comps]
-        + next_len * (sums[comps:2 * comps] - step_len * sums[2 * comps:3 * comps])
+        means[:comps] + along * means[comps:2 * comps]
+        + next_len * (means[comps:2 * comps] - step_len * means[2 * comps:3 * comps])
     )
 
     rows = jnp.transpose(pad_rows(total, LANES))
@@ -400,13 +411,16 @@
     row_copies = exchange(out_rows, in_rows, row_send, row_recv)
     sends += row_copies
     in_rows[group] = out_rows[group]
-    field_ref[0] = solved + along * residue + next_len * left
+    field_buf[0] = solved + along * residue + next_len * left
+    field_copy = pltpu.make_async_copy(field_buf, field_ref, output_sem)
+    field_copy.start()
     arrive(row_copies)
     back = jnp.transpose(in_rows[...].reshape(places, LANES))[:16]
     picked = jnp.dot(back, select, precision=HIGHEST, preferred_element_type=F32)
     stress_ref[...] = picked[:comps]
     for copy in sends:
         copy.wait_send()
+    field_copy.wait()
 
 
 def solution(mesh):
@@ -429,7 +443,7 @@
                 jax.ShapeDtypeStruct((1, dofs, columns), F32),
             ),
             in_specs=[hbm] * 6 + [pl.BlockSpec(memory_space=pltpu.SMEM)] + [hbm] * 3,
-            out_specs=(vmem, vmem),
+            out_specs=(vmem, hbm),
             scratch_shapes=[
                 pltpu.VMEM(deform.shape, F32),
                 pltpu.VMEM((1, points), jnp.int32),
@@ -450,14 +464,17 @@
                 pltpu.VMEM((2, block, columns), F32),
                 pltpu.VMEM((2, block, columns), F32),
                 pltpu.VMEM((parts, 48, LANES), F32),
+                pltpu.VMEM((parts, 8, columns), F32),
                 pltpu.VMEM((parts, 32, columns), F32),
                 pltpu.VMEM((parts, 8, columns), F32),
                 pltpu.VMEM((groups, padded, LANES), F32),
                 pltpu.VMEM((groups, padded, LANES), F32),
-                dma((9,)),
+                pltpu.VMEM((1, dofs, columns), F32),
+                dma((9,)), dma,
                 dma((groups - 1,)), dma((groups - 1,)),
                 dma((2,)), dma((2,)),
                 dma((2,)), dma((2,)),
+                dma((parts - 1,)), dma((parts - 1,)),
                 dma((parts - 1,)), dma((parts - 1,)),
                 dma((parts - 1,)), dma((parts - 1,)),
                 dma((parts - 1,)), dma((parts - 1,)),

time: 34.4 us -> 33.9 us (0.985)
  Pallas kernels: 30.6 us -> 30.1 us
    pallas_call x1, Pallas kernels: 30.6 us -> 30.1 us  [shards(): pl.pallas_call(functools.partial(kernel, groups, parts, capacity), out_sh...]
where the time goes in v3:
time: 33.9 us; the launch traced here: 33.7 us
  Pallas kernels  30.1 us (89%)
  local copies, waits for them, and re-layouts  2.91 us (9%)
  between operations  0.64 us (2%)
    pallas_call x1, Pallas kernels, shards(): pl.pallas_call(functools.partial(kernel, groups, parts, capacity), out_sh...  30.1 us
    unnamed x2, local copies, waits for them, and re-layouts  2.91 us

profile of v3, /device:TPU:0, one launch (start us, length us, event | category | flops | bytes accessed | tf_op | source)
XLA Modules:
  0.0 33.7 jit_solution(14665075928730643330)
XLA Ops:
  0.6 30.1 %shard_map.113 = (f32[9,64]{1,0:T(8,128)}, f32[1,384,128]{2,1,0:T(8,128)}) custom-call(f32[9,64]{1,0:T(8,128)} %deform_hbm.1, s32[1,64]{1,0:T(1,128)} %bitcast.8, s32[1,64]{1,0:T(1,128)} %bitcast.9, f32[1,384]{1,0:T(1,128)} %stiff_hbm.1, f32[1,384]{1,0:T(1,128)} %cubic_hbm.1, f32[1,6,2,64,64]{4,3,2,1,0:T(8,128)} %coupling_hbm.1, s32[1,2,6]{2,1,0:T(2,128)} %bitcast.7, ...), custom_call_target="tpu_custom_call" | custom-call | tf_op jit(solution)/shard_map/pallas_call | solution.py:439
  30.8 1.3 %copy.14 = f32[9,64]{1,0:T(8,128)} copy(f32[9,64]{1,0:T(8,128)} %get-tuple-element.4) | data formatting | bytes 4608
  32.1 1.6 %copy.15 = f32[1,384,128]{2,1,0:T(8,128)} copy(f32[1,384,128]{2,1,0:T(8,128)} %get-tuple-element.5) | data formatting | bytes 393216

commit v4 on v3

--- a/solution.py
+++ b/solution.py
@@ -215,10 +215,11 @@
         return jnp.concatenate([values[:, :block], values[:, dofs - block:]], axis=1)
 
     image_map = apply_rows(maps, stiff_high[...], stiff_low[...])
-    edge_out[0:16, :] = ends(maps)
-    edge_out[16:32, :] = ends(image_map)
-    edge_out[32:48, :] = ends(cubic)
-    edge_out[48:, :] = jnp.concatenate([own_edge[:block // 2], own_edge[block // 2:]], axis=1)
+    packed_rows = edge_out.shape[0] - block // 2
+    edge_out[:packed_rows, :] = pad_rows(
+        ends(jnp.concatenate([maps[:comps], image_map[:comps], cubic[:1]], axis=0)), packed_rows
+    )
+    edge_out[packed_rows:, :] = jnp.concatenate([own_edge[:block // 2], own_edge[block // 2:]], axis=1)
 
     pl.semaphore_wait(barrier, groups + parts - 2)
 
@@ -244,7 +245,7 @@
     average_high, average_low = split(pad_rows(average_ref[:, 0, :], 16))
 
     arrive(edge_copies)
-    packed = edge_in[1, 48:, :]
+    packed = edge_in[1, packed_rows:, :]
     next_spring = square_nt(jnp.concatenate([packed[:, :block], packed[:, block:]], axis=0))
     next_high, next_low = split(next_spring)
     high, low = split(stiffness[dofs - block:, dofs - block:] + next_spring)
@@ -257,7 +258,13 @@
     def next_rows(values):
         return apply_rows(values, next_high, next_low)
 
-    prev_edge, next_edge = edge_in[0], edge_in[1]
+    def unpack(values):
+        return jnp.concatenate([
+            pad_rows(values[:comps], 16), pad_rows(values[comps:2 * comps], 16),
+            pad_rows(values[2 * comps:2 * comps + 1], 16),
+        ], axis=0)
+
+    prev_edge, next_edge = unpack(edge_in[0, :packed_rows]), unpack(edge_in[1, :packed_rows])
     prev_map, next_map = prev_edge[0:16, block:], next_edge[0:16, :block]
     first_map, last_map = maps[:, :block], maps[:, dofs - block:]
     through_own = own_rows(jnp.concatenate([prev_map, first_map], axis=0))
@@ -276,11 +283,11 @@
         second_map[:, dofs - block:] - next_rows(next_image),
     ], axis=1)
     basis = jnp.concatenate([maps, image_map, second_map, cubic], axis=0)
-    gram_buf[part, 0:32] = dot_nt(
-        basis[0:32], jnp.concatenate([basis[0:48], jnp.zeros((LANES - 48, dofs), F32)], axis=0),
-        HIGHEST,
-    )
-    gram_buf[part, 32:48] = ends(second_map)
+    products = dot_nt(basis[0:32], basis[0:48], HIGHEST)
+    gram_buf[part, 0:16] = jnp.concatenate(
+        [products[0:16, 0:32], products[16:32, 16:48], jnp.zeros((16, LANES - 64), F32)], axis=1
+    )
+    gram_buf[part, 16:32] = ends(second_map)
     gram_copies = share(gram_buf, gram_send, gram_recv)
     sends += gram_copies
 
@@ -305,7 +312,7 @@
         jnp.concatenate([prev_map, next_map], axis=1),
         jnp.concatenate([prev_image, next_image], axis=1),
         jnp.concatenate(
-            [gram_buf[behind, 32:48][:, block:], gram_buf[after, 32:48][:, :block]], axis=1
+            [gram_buf[behind, 16:32][:, block:], gram_buf[after, 16:32][:, :block]], axis=1
         ),
         jnp.concatenate([prev_edge[32:48, block:], next_edge[32:48, :block]], axis=1),
     ], axis=0)
@@ -313,7 +320,7 @@
     ghost_hard = ghost_cols[:, 48:49] * flag
     gram = gathered(gram_buf)
     forms = jnp.concatenate(
-        [gram[0:16, 0:16], gram[0:16, 16:32], gram[16:32, 16:32], gram[16:32, 32:48]], axis=0
+        [gram[0:16, 0:16], gram[0:16, 16:32], gram[0:16, 32:48], gram[0:16, 48:64]], axis=0
     )
     forms = jnp.dot(forms, strain, precision=HIGHEST, preferred_element_type=F32)
     norm = col_sum(forms[0:16] * strain)
@@ -361,15 +368,15 @@
 
     image = coupled(apply_split(stiff_high[...], stiff_low[...], residue), ghost)
     image = image + tangent * residue
+    first_buf[part] = pad_rows(jnp.concatenate([
+        col_sum(residue * residue), col_sum(residue * image),
+    ], axis=0), first_buf.shape[1])
+    first_copies = share(first_buf, first_send, first_recv)
     halo_out[0] = image[:block]
     halo_out[1] = image[dofs - block:]
     halo_copies = to_neighbours(
         halo_out.at[0], halo_out.at[1], halo_in, halo_send, halo_recv
     )
-    first_buf[part] = pad_rows(jnp.concatenate([
-        col_sum(residue * residue), col_sum(residue * image),
-    ], axis=0), first_buf.shape[1])
-    first_copies = share(first_buf, first_send, first_recv)
     second = apply_split(stiff_high[...], stiff_low[...], image)
     mean_buf[part] = pad_rows(jnp.concatenate(
         [averaged(solved), averaged(residue), averaged(image)], axis=0
@@ -433,6 +440,7 @@
         capacity = 2 * points // groups
         columns = groups * capacity
         padded = -(-capacity // 8) * 8
+        edge_rows = -(-(2 * comps + 1) // 8) * 8
         vmem = pl.BlockSpec(memory_space=pltpu.VMEM)
         hbm = pl.BlockSpec(memory_space=pltpu.HBM)
         dma = pltpu.SemaphoreType.DMA
@@ -459,11 +467,11 @@
                 pltpu.VMEM((dofs, dofs), BF16),
                 pltpu.VMEM((groups, padded, LANES), F32),
                 pltpu.VMEM((groups, padded, LANES), F32),
-                pltpu.VMEM((48 + block // 2, LANES), F32),
-                pltpu.VMEM((2, 48 + block // 2, LANES), F32),
+                pltpu.VMEM((edge_rows + block // 2, LANES), F32),
+                pltpu.VMEM((2, edge_rows + block // 2, LANES), F32),
                 pltpu.VMEM((2, block, columns), F32),
                 pltpu.VMEM((2, block, columns), F32),
-                pltpu.VMEM((parts, 48, LANES), F32),
+                pltpu.VMEM((parts, 32, LANES), F32),
                 pltpu.VMEM((parts, 8, columns), F32),
                 pltpu.VMEM((parts, 32, columns), F32),
                 pltpu.VMEM((parts, 8, columns), F32),

time: 33.9 us -> 33.6 us (level)
  no operation moved by 1% of the time
where the time goes in v4:
time: 33.6 us; the launch traced here: 33.4 us
  Pallas kernels  29.8 us (89%)
  local copies, waits for them, and re-layouts  2.91 us (9%)
  between operations  0.64 us (2%)
    pallas_call x1, Pallas kernels, shards(): pl.pallas_call(functools.partial(kernel, groups, parts, capacity), out_sh...  29.8 us
    unnamed x2, local copies, waits for them, and re-layouts  2.91 us

profile of v4, /device:TPU:0, one launch (start us, length us, event | category | flops | bytes accessed | tf_op | source)
XLA Modules:
  0.0 33.4 jit_solution(1828751667856830309)
XLA Ops:
  0.6 29.8 %shard_map.113 = (f32[9,64]{1,0:T(8,128)}, f32[1,384,128]{2,1,0:T(8,128)}) custom-call(f32[9,64]{1,0:T(8,128)} %deform_hbm.1, s32[1,64]{1,0:T(1,128)} %bitcast.8, s32[1,64]{1,0:T(1,128)} %bitcast.9, f32[1,384]{1,0:T(1,128)} %stiff_hbm.1, f32[1,384]{1,0:T(1,128)} %cubic_hbm.1, f32[1,6,2,64,64]{4,3,2,1,0:T(8,128)} %coupling_hbm.1, s32[1,2,6]{2,1,0:T(2,128)} %bitcast.7, ...), custom_call_target="tpu_custom_call" | custom-call | tf_op jit(solution)/shard_map/pallas_call | solution.py:447
  30.5 1.3 %copy.14 = f32[9,64]{1,0:T(8,128)} copy(f32[9,64]{1,0:T(8,128)} %get-tuple-element.4) | data formatting | bytes 4608
  31.8 1.6 %copy.15 = f32[1,384,128]{2,1,0:T(8,128)} copy(f32[1,384,128]{2,1,0:T(8,128)} %get-tuple-element.5) | data formatting | bytes 393216
